TPU v7x, 512 devices: a whole 4x4x16 slice. The times are simulated.
512 devices in a mesh: rep: 4 (over x), fsdp: 16 (over z), tp: 8 (over y, core).
Axes of the slice: x: 4, y: 4, z: 16, core: 2. Of those that a mesh axis runs over, the one named last changes fastest.
Arguments:
- tracker: bfloat16 [4, 4096, 14336], P('rep', 'fsdp', 'tp'), may hold values from -20 to 20
- grad_delta: bfloat16 [4, 4096, 14336], P('rep', 'fsdp', 'tp'), may hold values from -20 to 20
- momentum: bfloat16 [4, 4096, 14336], P('rep', 'fsdp', 'tp'), may hold values from -20 to 20
- q_basis: bfloat16 [4, 14336, 512], P('rep', 'tp', 'fsdp'), may hold values from -0.046875 to 0.046875
- mix_counts: int32 [4, 3], replicated, may hold values from 1 to 8
Outputs:
- new_tracker: bfloat16 [4, 4096, 14336], P('rep', 'fsdp', 'tp')
- new_momentum: bfloat16 [4, 4096, 14336], P('rep', 'fsdp', 'tp')
- left_basis: bfloat16 [4, 4096, 512], P('rep', 'fsdp')
- q_new: bfloat16 [4, 14336, 512], P('rep', 'tp', 'fsdp')
All inputs are finite; a program needn't handle non-finite values.
Results may differ from a plain program's by a relative error of at most 0.0061.
Values may be sent and summed in bfloat16 or wider, within the bound.
A program may use at most 64 MiB of HBM per device.

v0:
```python
import jax
import jax.numpy as jnp
from jax import lax
from jax.sharding import PartitionSpec as P

D = 4096
FF = 14336


def extended(block, sides, width):
    for axis, dim in sides:
        count = lax.axis_size(axis)
        forward = [(i, i + 1) for i in range(count - 1)]
        forward.append((count - 1, 0))
        backward = [(target, source) for source, target in forward]
        low = lax.ppermute(
            lax.slice_in_dim(block, block.shape[dim] - width, None, axis=dim), axis, forward
        )
        high = lax.ppermute(lax.slice_in_dim(block, 0, width, axis=dim), axis, backward)
        block = jnp.concatenate([low, block, high], axis=dim)
    return block


def orthonormal(pmat, gram):
    factor = jnp.linalg.cholesky(gram)
    solved = jax.scipy.linalg.solve_triangular(factor, pmat.T, lower=True).T
    return (solved * jnp.sqrt(jnp.float32(D))).astype(jnp.bfloat16)


def local(tracker, grad_delta, momentum, q_basis, mix_counts):
    agent = lax.axis_index("rep")
    counts = mix_counts.astype(jnp.float32)
    select = (jnp.arange(counts.shape[0]) == agent).astype(jnp.float32)
    mine = jnp.sum(select[:, None] * counts, axis=0)
    weights = mine / jnp.sum(mine)
    near = extended(tracker, (("rep", 0),), 1)
    mixed = (
        weights[0] * near[1].astype(jnp.float32)
        + weights[1] * near[0].astype(jnp.float32)
        + weights[2] * near[2].astype(jnp.float32)
    )
    tracked = mixed + grad_delta[0].astype(jnp.float32)
    new_tracker = tracked.astype(jnp.bfloat16)
    accum = momentum[0].astype(jnp.float32) + tracked
    accum_b = accum.astype(jnp.bfloat16)
    scale = 1.0 / jnp.sqrt(jnp.float32(D))
    basis_full = lax.all_gather(q_basis, "fsdp", axis=2, tiled=True)[0]
    partial_left = jnp.dot(accum_b, basis_full, preferred_element_type=jnp.float32)
    pmat = lax.psum(partial_left, "tp")
    gram_part = jnp.dot(pmat.T, pmat, precision=lax.Precision.HIGHEST)
    gram = lax.psum(gram_part, "fsdp")
    left_b = orthonormal(pmat, gram)
    block = left_b
    product = lax.dot_general(
        block, accum_b, (((0,), (0,)), ((), ())), preferred_element_type=jnp.float32
    )
    right_t = lax.psum_scatter(product * scale, "fsdp", scatter_dimension=0, tiled=True)
    squares = lax.psum(jnp.sum(right_t * right_t, axis=1), "tp")
    rms = jnp.sqrt(squares / FF) + 1e-06
    q_new = (right_t / rms[:, None]).T.astype(jnp.bfloat16)
    right_b = right_t.astype(jnp.bfloat16)
    block = left_b
    feed = jnp.dot(
        block,
        lax.all_gather(right_b, "fsdp", axis=0, tiled=True),
        preferred_element_type=jnp.float32,
    )
    new_momentum = (accum - 0.5 * scale * feed).astype(jnp.bfloat16)
    return (new_tracker[None], new_momentum[None], left_b[None], q_new[None])


def solution(mesh):
    in_specs = (
        P("rep", "fsdp", "tp"),
        P("rep", "fsdp", "tp"),
        P("rep", "fsdp", "tp"),
        P("rep", "tp", "fsdp"),
        P(),
    )
    out_specs = (
        P("rep", "fsdp", "tp"),
        P("rep", "fsdp", "tp"),
        P("rep", "fsdp", None),
        P("rep", "tp", "fsdp"),
    )
    return jax.shard_map(local, mesh=mesh, in_specs=in_specs, out_specs=out_specs, check_vma=False)
```

profile of v0, /device:TPU:2, one launch (start us, length us, event | category | flops | bytes accessed | tf_op | source)
XLA Modules:
  0.0 640.5 jit_solution(14598845073682928262)
XLA Ops:
  7.2 0.7 all-gather.3.cloned.1.call-update
  7.9 7.8 %collective-permute-start.1 = (bf16[1,256,1792]{2,1,0:T(8,128)(2,1)}, bf16[1,256,1792]{2,1,0:T(8,128)(2,1)S(1)}, u32[]{:S(2)}, u32[]{:S(2)}) collective-permute-start(bf16[1,256,1792]{2,1,0:T(8,128)(2,1)} %param.5), channel_id=1, source_target_pairs={{128,0},{256,128},{384,256},{0,384},{129,1},{257,129},{385,257},{1... | collective-permute-start | bytes 2752520 | tf_op jit(solution)/shard_map/ppermute | solution.py:19
  15.8 1.9 collective-permute-start
  17.7 1.4 fusion.37
  19.1 0.6 broadcast_divide_fusion
  19.7 0.6 fusion.46
  20.3 11.8 %collective-permute-done.1 = bf16[1,256,1792]{2,1,0:T(8,128)(2,1)S(1)} collective-permute-done((bf16[1,256,1792]{2,1,0:T(8,128)(2,1)}, bf16[1,256,1792]{2,1,0:T(8,128)(2,1)S(1)}, u32[]{:S(2)}, u32[]{:S(2)}) %collective-permute-start.1) | collective-permute-done | bytes 917536 | tf_op jit(solution)/shard_map/ppermute | solution.py:19
  32.1 3.2 collective-permute-done
  35.3 0.9 copy-done.6
  36.3 5.5 fusion.44
  41.8 45.7 %all-gather.3.cloned.1.call-done = bf16[1,1792,512]{1,2,0:T(8,128)(2,1)} async-done(((bf16[1,1792,32]{1,2,0:T(8,128)(2,1)}), bf16[1,1792,512]{1,2,0:T(8,128)(2,1)}) %all-gather.3.cloned.1.call-update) | async-done | bytes 1835024 | tf_op jit(solution)/shard_map/all_gather | solution.py:47
  87.5 3.0 fusion.3
  90.6 73.0 %all-reduce.4.cloned.1.call-done = f32[256,512]{1,0:T(8,128)} async-done(((f32[256,512]{1,0:T(8,128)}), f32[256,512]{1,0:T(8,128)}) %all-reduce.4.cloned.1.call-update) | async-done | bytes 524304 | tf_op jit(solution)/shard_map/psum | solution.py:49
  163.6 3.3 fusion.47
  167.1 138.0 %all-reduce.6.cloned.1.call-done = f32[512,512]{0,1:T(8,128)} async-done(((f32[512,512]{0,1:T(8,128)}), f32[512,512]{0,1:T(8,128)}) %all-reduce.6.cloned.1.call-update) | async-done | bytes 1048592 | tf_op jit(solution)/shard_map/psum | solution.py:51
  305.1 2.6 copy.10
  307.7 1.8 fusion.5
  309.5 1.0 copy-done.4
  310.5 11.7 %cholesky.104 = f32[128,128]{1,0:T(8,128)S(1)} custom-call(f32[128,128]{1,0:T(8,128)S(1)} %cholesky.266), custom_call_target="Cholesky" | custom-call | tf_op jit(solution)/shard_map/jit(cholesky)/cholesky | solution.py:25
  322.2 1.2 cholesky.224
  323.4 9.8 %custom-call.31 = f32[1,128,128]{1,2,0:T(8,128)S(1)} custom-call(f32[1,128,128]{2,1,0:T(8,128)S(1)} %get-tuple-element.41), custom_call_target="InvertDiagBlocksLowerTriangular" | custom-call | tf_op jit(solution)/shard_map/jit(cholesky)/cholesky | solution.py:25
  333.2 2.0 constant_dynamic-update-slice_fusion.3
  335.2 1.2 convolution_subtract_fusion
  336.5 11.7 %cholesky.217 = f32[128,128]{1,0:T(8,128)S(1)} custom-call(f32[128,128]{1,0:T(8,128)S(1)} %cholesky.270), custom_call_target="Cholesky" | custom-call | tf_op jit(solution)/shard_map/jit(cholesky)/cholesky | solution.py:25
  348.2 0.6 select_reduce_fusion.2
  348.8 10.0 %custom-call.32 = f32[1,128,128]{1,2,0:T(8,128)S(1)} custom-call(f32[1,128,128]{2,1,0:T(8,128)S(1)} %get-tuple-element.38), custom_call_target="InvertDiagBlocksLowerTriangular" | custom-call | tf_op jit(solution)/shard_map/jit(cholesky)/cholesky | solution.py:25
  358.8 0.9 convolution_dynamic-update-slice_fusion
  359.8 1.4 convolution_subtract_fusion.3
  361.2 11.7 %cholesky.238 = f32[128,128]{1,0:T(8,128)S(1)} custom-call(f32[128,128]{1,0:T(8,128)S(1)} %cholesky.275), custom_call_target="Cholesky" | custom-call | tf_op jit(solution)/shard_map/jit(cholesky)/cholesky | solution.py:25
  372.9 0.6 select_reduce_fusion.1
  373.6 9.8 %custom-call.33 = f32[1,128,128]{1,2,0:T(8,128)S(1)} custom-call(f32[1,128,128]{2,1,0:T(8,128)S(1)} %get-tuple-element.35), custom_call_target="InvertDiagBlocksLowerTriangular" | custom-call | tf_op jit(solution)/shard_map/jit(cholesky)/cholesky | solution.py:25
  383.4 0.8 convolution_dynamic-update-slice_fusion.1
  384.2 1.4 convolution_subtract_fusion.5
  385.6 11.7 %cholesky.255 = f32[128,128]{1,0:T(8,128)S(1)} custom-call(f32[128,128]{1,0:T(8,128)S(1)} %convolution_subtract_fusion.5), custom_call_target="Cholesky" | custom-call | tf_op jit(solution)/shard_map/jit(cholesky)/cholesky | solution.py:25
  397.3 0.7 select_reduce_fusion
  398.0 0.7 compare_reduce_fusion.1
  398.7 0.6 compare_reduce_fusion
  399.3 0.7 compare_reduce_fusion.2
  402.5 2.6 select_select_fusion
  405.1 14.5 %while.1 = (s32[]{:T(128)}, f32[512,512]{1,0:T(8,128)}, s32[4,2]{0,1:T(2,128)S(1)}, f32[4,128,128]{2,1,0:T(8,128)}, s32[]{:T(128)}) while((s32[]{:T(128)}, f32[512,512]{1,0:T(8,128)}, s32[4,2]{0,1:T(2,128)S(1)}, f32[4,128,128]{2,1,0:T(8,128)}, s32[]{:T(128)}) %tuple.37), condition=%wide.while_cond, body=%wide.while_body.sunk | while | flops 2 | bytes 132205 | solution.py:26
  405.2 0.6 fusion.57
  405.8 3.0 bitcast_dynamic-update-slice_fusion.2
  408.9 0.6 fusion.57
  409.4 3.0 bitcast_dynamic-update-slice_fusion.2
  412.5 0.6 fusion.57
  413.1 3.0 bitcast_dynamic-update-slice_fusion.2
  416.1 0.6 fusion.57
  416.7 2.9 bitcast_dynamic-update-slice_fusion.2
  419.6 40.8 %custom-call.34 = f32[4,128,128]{1,2,0:T(8,128)} custom-call(f32[4,128,128]{2,1,0:T(8,128)} %get-tuple-element.11), custom_call_target="InvertDiagBlocksLowerTriangular" | custom-call | tf_op jit(solution)/shard_map/jit(_solve_triangular)/triangular_solve | solution.py:26
  460.4 1.1 fusion.23
  461.5 1.2 convolution_subtract_fusion.4
  462.8 1.2 fusion.31
  463.9 1.5 convolution_subtract_fusion.2
  465.4 1.2 fusion.29
  466.6 1.8 convolution_subtract_fusion.1
  468.4 1.2 fusion.28
  469.6 2.5 convolution_multiply_fusion
  472.1 75.2 %reduce-scatter.2.cloned.1.call-done = f32[32,1792]{1,0:T(8,128)} async-done(((f32[512,1792]{1,0:T(8,128)}), f32[32,1792]{1,0:T(8,128)}) %reduce-scatter.2.cloned.1.call-update) | async-done | bytes 229392 | tf_op jit(solution)/shard_map/reduce_scatter | solution.py:57
  547.3 1.1 multiply_reduce_fusion
  548.4 12.4 %psum.23 = f32[32]{0:T(128)S(1)} all-reduce(f32[32]{0:T(128)S(1)} %multiply_reduce_fusion), channel_id=1, replica_groups=mesh['rep'=4,'fsdp'=16,'tp'=8] {'tp'}, use_global_device_ids=true, to_apply=%region_14.15 | all-reduce | flops 32 | bytes 256 | tf_op jit(solution)/shard_map/psum | solution.py:58
  560.8 1.8 fusion.27
  562.7 0.8 copy.11
  563.5 67.4 %all-gather.5.cloned.1.call-done = bf16[512,1792]{1,0:T(8,128)(2,1)} async-done(((bf16[32,1792]{1,0:T(8,128)(2,1)}), bf16[512,1792]{1,0:T(8,128)(2,1)}) %all-gather.5.cloned.1.call-update) | async-done | bytes 1835024 | tf_op jit(solution)/shard_map/all_gather | solution.py:65
  630.9 3.1 fusion.2
  (35 shorter events, 0.9 us)
Async XLA Ops:
  7.2 80.3 %all-gather.3.cloned.1.call-start = ((), (), s32[]{:S(2)}) async-start(), calls=%async_computation.1 | async-start | bytes 1949696 | tf_op jit(solution)/shard_map/all_gather | solution.py:47
  7.9 155.7 %all-reduce.4.cloned.1.call-start = ((), (), s32[]{:S(2)}) async-start(), calls=%async_computation.2 | async-start | bytes 1048576 | tf_op jit(solution)/shard_map/psum | solution.py:49
  7.9 24.2 %collective-permute-start.1 = (bf16[1,256,1792]{2,1,0:T(8,128)(2,1)}, bf16[1,256,1792]{2,1,0:T(8,128)(2,1)S(1)}, u32[]{:S(2)}, u32[]{:S(2)}) collective-permute-start(bf16[1,256,1792]{2,1,0:T(8,128)(2,1)} %param.5), channel_id=1, source_target_pairs={{128,0},{256,128},{384,256},{0,384},{129,1},{257,129},{385,257},{1... | collective-permute-start | bytes 2752520 | tf_op jit(solution)/shard_map/ppermute | solution.py:19
  15.8 19.6 %collective-permute-start = (bf16[1,256,1792]{2,1,0:T(8,128)(2,1)}, bf16[1,256,1792]{2,1,0:T(8,128)(2,1)S(1)}, u32[]{:S(2)}, u32[]{:S(2)}) collective-permute-start(bf16[1,256,1792]{2,1,0:T(8,128)(2,1)} %param.5), channel_id=1, source_target_pairs={{0,128},{128,256},{256,384},{384,0},{1,129},{129,257},{257,385},{3... | collective-permute-start | bytes 2752520 | tf_op jit(solution)/shard_map/ppermute | solution.py:16
  32.1 3.2 copy-start.5
  35.3 0.9 copy-start.6
  36.3 51.2 %copy-start = (bf16[1,256,1792]{2,1,0:T(8,128)(2,1)S(1)}, bf16[1,256,1792]{2,1,0:T(8,128)(2,1)}, u32[]{:S(2)}) copy-start(bf16[1,256,1792]{2,1,0:T(8,128)(2,1)} %param.7) | copy-start | bytes 2752516
  90.5 214.6 %all-reduce.6.cloned.1.call-start = ((), (), s32[]{:S(2)}) async-start(), calls=%async_computation.3 | async-start | bytes 2097152 | tf_op jit(solution)/shard_map/psum | solution.py:51
  166.9 380.4 %reduce-scatter.2.cloned.1.call-start = ((), (), s32[]{:S(2)}) async-start(), calls=%async_computation.4 | async-start | bytes 3899392 | tf_op jit(solution)/shard_map/reduce_scatter | solution.py:57
  309.5 1.0 copy-start.4
  373.6 86.8 %copy-start.1 = (f32[256,512]{1,0:T(8,128)S(1)}, f32[256,512]{1,0:T(8,128)}, u32[]{:S(2)}) copy-start(f32[256,512]{1,0:T(8,128)} %all-reduce.4.cloned.1.call-done) | copy-start | bytes 1572868
  466.6 3.0 copy-start.2
  472.0 90.6 %copy-start.3 = (f32[128,256]{1,0:T(8,128)S(1)}, f32[128,256]{1,0:T(8,128)}, u32[]{:S(2)}) copy-start(f32[128,256]{1,0:T(8,128)} %copy-done.2) | copy-start | bytes 393220
  472.1 158.8 %all-gather.5.cloned.1.call-start = ((), (), s32[]{:S(2)}) async-start(), calls=%async_computation.5 | async-start | bytes 1949696 | tf_op jit(solution)/shard_map/all_gather | solution.py:65
Sparse Core Ops, SparseCore 0:
  10.1 77.3 all-gather.2
  90.6 72.8 all-reduce.3
  167.0 138.0 all-reduce.5
  472.2 75.0 reduce-scatter.1
  562.7 68.1 all-gather.4
where the time goes:
time: 642 us; the launch traced here: 641 us
  waiting for transfers between devices  415 us (65%)
  other arithmetic  136 us (21%)
  matrix products  28.8 us (4%)
  local copies, waits for them, and re-layouts  21.6 us (3%)
  between operations  16.5 us (3%)
  blocking collectives  12.4 us (2%)
  starting transfers between devices  10.1 us (2%)
    psum x1, waiting for transfers between devices, local(): gram = lax.psum(gram_part, 'fsdp')  138 us
    another operation x14, other arithmetic, orthonormal(): factor = jnp.linalg.cholesky(gram)  80.4 us
    reduce_scatter x1, waiting for transfers between devices, local(): lax.psum_scatter(product * scale, 'fsdp', scatter_dimension=0, tiled=True)  75.2 us
    psum x1, waiting for transfers between devices, local(): pmat = lax.psum(partial_left, 'tp')  73 us
    all_gather x1, waiting for transfers between devices, local(): lax.all_gather(right_b, 'fsdp', axis=0, tiled=True)  67.4 us
    all_gather x1, waiting for transfers between devices, local(): basis_full = lax.all_gather(q_basis, 'fsdp', axis=2, tiled=True)[0]  45.7 us
    another operation x3, other arithmetic, orthonormal(): solved = jax.scipy.linalg.solve_triangular(factor, pmat.T, lower=True).T  43.4 us
    another operation x12, local copies, waits for them, and re-layouts  14.5 us
  transfers between devices with their start and end apart: 7, of which 7 were waited for; matrix products, arithmetic and copies ran while one was open for 1% of the time, Pallas kernels for 0%

commit v1 on v0

--- a/solution.py
+++ b/solution.py
@@ -48,7 +48,7 @@
     partial_left = jnp.dot(accum_b, basis_full, preferred_element_type=jnp.float32)
     pmat = lax.psum(partial_left, "tp")
     gram_part = jnp.dot(pmat.T, pmat, precision=lax.Precision.HIGHEST)
-    gram = lax.psum(gram_part, "fsdp")
+    gram = jnp.sum(lax.all_gather(gram_part, "fsdp"), axis=0)
     left_b = orthonormal(pmat, gram)
     block = left_b
     product = lax.dot_general(

time: 642 us -> 700 us (1.090)
  waiting for transfers between devices: 415 us -> 468 us
  other arithmetic: 136 us -> 143 us
    all_gather x0 -> x1, waiting for transfers between devices: none -> 189 us  [local(): gram = jnp.sum(lax.all_gather(gram_part, 'fsdp'), axis=0)]
    psum x1 -> x0, waiting for transfers between devices: 138 us -> none  [local(): gram = lax.psum(gram_part, 'fsdp')]
    ppermute x1, waiting for transfers between devices: 11.8 us -> 3.13 us  [extended(): lax.ppermute(lax.slice_in_dim(block, 0, width, axis=dim), axis, backward)]
    ppermute x1, waiting for transfers between devices: 3.2 us -> 11.8 us  [extended(): lax.ppermute(lax.slice_in_dim(block, block.shape[dim] - width, None, axis...]
    reduce_sum x0 -> x1, other arithmetic: none -> 7.91 us  [local(): gram = jnp.sum(lax.all_gather(gram_part, 'fsdp'), axis=0)]
where the time goes in v1:
time: 700 us; the launch traced here: 696 us
  waiting for transfers between devices  468 us (67%)
  other arithmetic  143 us (20%)
  matrix products  27.2 us (4%)
  local copies, waits for them, and re-layouts  18.8 us (3%)
  between operations  16.9 us (2%)
  blocking collectives  12.4 us (2%)
  starting transfers between devices  10.2 us (1%)
    all_gather x1, waiting for transfers between devices, local(): gram = jnp.sum(lax.all_gather(gram_part, 'fsdp'), axis=0)  189 us
    another operation x14, other arithmetic, orthonormal(): factor = jnp.linalg.cholesky(gram)  81.2 us
    reduce_scatter x1, waiting for transfers between devices, local(): lax.psum_scatter(product * scale, 'fsdp', scatter_dimension=0, tiled=True)  76.6 us
    psum x1, waiting for transfers between devices, local(): pmat = lax.psum(partial_left, 'tp')  73 us
    all_gather x1, waiting for transfers between devices, local(): lax.all_gather(right_b, 'fsdp', axis=0, tiled=True)  67.3 us
    all_gather x1, waiting for transfers between devices, local(): basis_full = lax.all_gather(q_basis, 'fsdp', axis=2, tiled=True)[0]  45.6 us
    another operation x3, other arithmetic, orthonormal(): solved = jax.scipy.linalg.solve_triangular(factor, pmat.T, lower=True).T  42 us
    another operation x12, local copies, waits for them, and re-layouts  14 us
  transfers between devices with their start and end apart: 7, of which 7 were waited for; matrix products, arithmetic and copies ran while one was open for 1% of the time, Pallas kernels for 0%

profile of v1, /device:TPU:2, one launch (start us, length us, event | category | flops | bytes accessed | tf_op | source)
XLA Modules:
  0.0 696.0 jit_solution(6097947939696439196)
XLA Ops:
  7.2 0.7 all-gather.5.cloned.1.call-update
  7.9 3.4 collective-permute-start
  11.4 6.3 collective-permute-start.1
  17.7 1.4 fusion.37
  19.1 0.6 broadcast_divide_fusion
  19.7 0.6 fusion.46
  20.3 11.8 %collective-permute-done = bf16[1,256,1792]{2,1,0:T(8,128)(2,1)S(1)} collective-permute-done((bf16[1,256,1792]{2,1,0:T(8,128)(2,1)}, bf16[1,256,1792]{2,1,0:T(8,128)(2,1)S(1)}, u32[]{:S(2)}, u32[]{:S(2)}) %collective-permute-start) | collective-permute-done | bytes 917536 | tf_op jit(solution)/shard_map/ppermute | solution.py:16
  32.1 3.1 collective-permute-done.1
  35.3 0.9 copy-done.7
  36.2 5.5 fusion.44
  41.7 45.6 %all-gather.5.cloned.1.call-done = bf16[1,1792,512]{1,2,0:T(8,128)(2,1)} async-done(((bf16[1,1792,32]{1,2,0:T(8,128)(2,1)}), bf16[1,1792,512]{1,2,0:T(8,128)(2,1)}) %all-gather.5.cloned.1.call-update) | async-done | bytes 1835024 | tf_op jit(solution)/shard_map/all_gather | solution.py:47
  87.3 3.0 fusion.3
  90.4 73.0 %all-reduce.3.cloned.1.call-done = f32[256,512]{1,0:T(8,128)} async-done(((f32[256,512]{1,0:T(8,128)}), f32[256,512]{1,0:T(8,128)}) %all-reduce.3.cloned.1.call-update) | async-done | bytes 524304 | tf_op jit(solution)/shard_map/psum | solution.py:49
  163.4 3.2 fusion.47
  166.6 0.3 reduce-scatter.2.cloned.1.call-start
  166.9 189.3 %all-gather.9.cloned.1.call-done = f32[8192,512]{1,0:T(8,128)} async-done(((f32[512,512]{1,0:T(8,128)}), f32[8192,512]{1,0:T(8,128)}) %all-gather.9.cloned.1.call-update) | async-done | bytes 16777232 | tf_op jit(solution)/shard_map/all_gather | solution.py:51
  356.2 7.9 %reduce_sum.38 = f32[512,512]{1,0:T(8,128)S(1)} reduce(f32[16,512,512]{2,1,0:T(8,128)} %bitcast.76, f32[]{:T(128)} %constant.151.clone.1), dimensions={0}, to_apply=%region_3.0 | reduce | flops 3932160 | bytes 17825796 | tf_op jit(solution)/shard_map/reduce_sum | solution.py:51
  364.1 1.3 copy.11
  365.5 1.4 fusion.5
  366.9 1.0 copy-done.5
  367.9 11.7 %cholesky.104 = f32[128,128]{1,0:T(8,128)S(1)} custom-call(f32[128,128]{1,0:T(8,128)S(1)} %cholesky.266), custom_call_target="Cholesky" | custom-call | tf_op jit(solution)/shard_map/jit(cholesky)/cholesky | solution.py:25
  379.7 0.1 cholesky.224
  379.8 9.8 %custom-call.31 = f32[1,128,128]{1,2,0:T(8,128)S(1)} custom-call(f32[1,128,128]{2,1,0:T(8,128)S(1)} %get-tuple-element.45), custom_call_target="InvertDiagBlocksLowerTriangular" | custom-call | tf_op jit(solution)/shard_map/jit(cholesky)/cholesky | solution.py:25
  389.6 1.2 constant_dynamic-update-slice_fusion.3
  390.9 1.3 convolution_subtract_fusion
  392.1 12.2 %cholesky.217 = f32[128,128]{1,0:T(8,128)S(1)} custom-call(f32[128,128]{1,0:T(8,128)S(1)} %cholesky.270), custom_call_target="Cholesky" | custom-call | tf_op jit(solution)/shard_map/jit(cholesky)/cholesky | solution.py:25
  404.3 9.8 %custom-call.32 = f32[1,128,128]{1,2,0:T(8,128)S(1)} custom-call(f32[1,128,128]{2,1,0:T(8,128)S(1)} %get-tuple-element.42), custom_call_target="InvertDiagBlocksLowerTriangular" | custom-call | tf_op jit(solution)/shard_map/jit(cholesky)/cholesky | solution.py:25
  414.2 0.3 convolution_dynamic-update-slice_fusion
  414.4 1.3 convolution_subtract_fusion.3
  415.7 11.7 %cholesky.238 = f32[128,128]{1,0:T(8,128)S(1)} custom-call(f32[128,128]{1,0:T(8,128)S(1)} %cholesky.275), custom_call_target="Cholesky" | custom-call | tf_op jit(solution)/shard_map/jit(cholesky)/cholesky | solution.py:25
  427.4 0.7 select_reduce_fusion.1
  428.1 0.7 compare_reduce_fusion.1
  428.8 11.3 %custom-call.33 = f32[1,128,128]{1,2,0:T(8,128)} custom-call(f32[1,128,128]{2,1,0:T(8,128)} %get-tuple-element.39), custom_call_target="InvertDiagBlocksLowerTriangular" | custom-call | tf_op jit(solution)/shard_map/jit(cholesky)/cholesky | solution.py:25
  440.1 1.0 convolution_dynamic-update-slice_fusion.1
  441.1 1.2 convolution_subtract_fusion.5
  442.4 11.9 %cholesky.255 = f32[128,128]{1,0:T(8,128)S(1)} custom-call(f32[128,128]{1,0:T(8,128)S(1)} %convolution_subtract_fusion.5), custom_call_target="Cholesky" | custom-call | tf_op jit(solution)/shard_map/jit(cholesky)/cholesky | solution.py:25
  454.3 0.7 compare_reduce_fusion
  455.0 0.6 compare_reduce_fusion.2
  458.3 1.1 select_select_fusion
  459.4 14.0 %while.1 = (s32[]{:T(128)}, f32[512,512]{1,0:T(8,128)}, s32[4,2]{0,1:T(2,128)S(1)}, f32[4,128,128]{2,1,0:T(8,128)}, s32[]{:T(128)}) while((s32[]{:T(128)}, f32[512,512]{1,0:T(8,128)}, s32[4,2]{0,1:T(2,128)S(1)}, f32[4,128,128]{2,1,0:T(8,128)}, s32[]{:T(128)}) %tuple.38), condition=%wide.while_cond, body=%wide.while_body.sunk | while | flops 2 | bytes 132705 | solution.py:26
  459.5 0.5 fusion.57
  460.0 2.9 bitcast_dynamic-update-slice_fusion.2
  463.0 0.5 fusion.57
  463.5 2.9 bitcast_dynamic-update-slice_fusion.2
  466.5 0.5 fusion.57
  467.1 2.9 bitcast_dynamic-update-slice_fusion.2
  470.1 0.5 fusion.57
  470.6 2.9 bitcast_dynamic-update-slice_fusion.2
  473.4 40.8 %custom-call.34 = f32[4,128,128]{1,2,0:T(8,128)} custom-call(f32[4,128,128]{2,1,0:T(8,128)} %get-tuple-element.11), custom_call_target="InvertDiagBlocksLowerTriangular" | custom-call | tf_op jit(solution)/shard_map/jit(_solve_triangular)/triangular_solve | solution.py:26
  514.3 1.1 fusion.23
  515.4 1.2 convolution_subtract_fusion.4
  516.7 1.2 fusion.31
  517.8 1.5 convolution_subtract_fusion.2
  519.3 1.2 fusion.29
  520.5 1.8 convolution_subtract_fusion.1
  522.3 1.2 fusion.28
  523.5 2.5 convolution_multiply_fusion
  526.0 76.6 %reduce-scatter.2.cloned.1.call-done = f32[32,1792]{1,0:T(8,128)} async-done(((f32[512,1792]{1,0:T(8,128)}), f32[32,1792]{1,0:T(8,128)}) %reduce-scatter.2.cloned.1.call-update) | async-done | bytes 229392 | tf_op jit(solution)/shard_map/reduce_scatter | solution.py:57
  602.6 1.1 multiply_reduce_fusion
  603.7 12.4 %psum.15 = f32[32]{0:T(128)S(1)} all-reduce(f32[32]{0:T(128)S(1)} %multiply_reduce_fusion), channel_id=1, replica_groups=mesh['rep'=4,'fsdp'=16,'tp'=8] {'tp'}, use_global_device_ids=true, to_apply=%region_14.15 | all-reduce | flops 32 | bytes 256 | tf_op jit(solution)/shard_map/psum | solution.py:58
  616.1 1.8 fusion.27
  618.0 0.8 copy.12
  618.9 67.3 %all-gather.7.cloned.1.call-done = bf16[512,1792]{1,0:T(8,128)(2,1)} async-done(((bf16[32,1792]{1,0:T(8,128)(2,1)}), bf16[512,1792]{1,0:T(8,128)(2,1)}) %all-gather.7.cloned.1.call-update) | async-done | bytes 1835024 | tf_op jit(solution)/shard_map/all_gather | solution.py:65
  686.2 3.1 fusion.2
  (38 shorter events, 0.7 us)
Async XLA Ops:
  7.2 80.1 %all-gather.5.cloned.1.call-start = ((), (), s32[]{:S(2)}) async-start(), calls=%async_computation.1 | async-start | bytes 1949696 | tf_op jit(solution)/shard_map/all_gather | solution.py:47
  7.9 155.5 %all-reduce.3.cloned.1.call-start = ((), (), s32[]{:S(2)}) async-start(), calls=%async_computation.2 | async-start | bytes 1048576 | tf_op jit(solution)/shard_map/psum | solution.py:49
  7.9 24.2 %collective-permute-start = (bf16[1,256,1792]{2,1,0:T(8,128)(2,1)}, bf16[1,256,1792]{2,1,0:T(8,128)(2,1)S(1)}, u32[]{:S(2)}, u32[]{:S(2)}) collective-permute-start(bf16[1,256,1792]{2,1,0:T(8,128)(2,1)} %param.5), channel_id=1, source_target_pairs={{0,128},{128,256},{256,384},{384,0},{1,129},{129,257},{257,385},{3... | collective-permute-start | bytes 2752520 | tf_op jit(solution)/shard_map/ppermute | solution.py:16
  11.4 23.9 %collective-permute-start.1 = (bf16[1,256,1792]{2,1,0:T(8,128)(2,1)}, bf16[1,256,1792]{2,1,0:T(8,128)(2,1)S(1)}, u32[]{:S(2)}, u32[]{:S(2)}) collective-permute-start(bf16[1,256,1792]{2,1,0:T(8,128)(2,1)} %param.5), channel_id=1, source_target_pairs={{128,0},{256,128},{384,256},{0,384},{129,1},{257,129},{385,257},{1... | collective-permute-start | bytes 2752520 | tf_op jit(solution)/shard_map/ppermute | solution.py:19
  32.1 3.1 copy-start.6
  35.3 0.9 copy-start.7
  36.2 51.1 %copy-start = (bf16[1,256,1792]{2,1,0:T(8,128)(2,1)S(1)}, bf16[1,256,1792]{2,1,0:T(8,128)(2,1)}, u32[]{:S(2)}) copy-start(bf16[1,256,1792]{2,1,0:T(8,128)(2,1)} %param.7) | copy-start | bytes 2752516
  90.3 265.9 %all-gather.9.cloned.1.call-start = ((), (), s32[]{:S(2)}) async-start(), calls=%async_computation.5 | async-start | bytes 17825792 | tf_op jit(solution)/shard_map/all_gather | solution.py:51
  166.6 436.1 %reduce-scatter.2.cloned.1.call-start = ((), (), s32[]{:S(2)}) async-start(), calls=%async_computation.3 | async-start | bytes 3899392 | tf_op jit(solution)/shard_map/reduce_scatter | solution.py:57
  366.9 1.0 copy-start.5
  428.1 86.2 %copy-start.2 = (f32[256,512]{1,0:T(8,128)S(1)}, f32[256,512]{1,0:T(8,128)}, u32[]{:S(2)}) copy-start(f32[256,512]{1,0:T(8,128)} %all-reduce.3.cloned.1.call-done) | copy-start | bytes 1572868
  473.4 50.0 %copy-start.1 = (bf16[1,256,1792]{2,1,0:T(8,128)(2,1)S(1)}, bf16[1,256,1792]{2,1,0:T(8,128)(2,1)}, u32[]{:S(2)}) copy-start(bf16[1,256,1792]{2,1,0:T(8,128)(2,1)} %param.7) | copy-start | bytes 2752516
  520.5 3.0 copy-start.3
  526.0 92.0 %copy-start.4 = (f32[128,256]{1,0:T(8,128)S(1)}, f32[128,256]{1,0:T(8,128)}, u32[]{:S(2)}) copy-start(f32[128,256]{1,0:T(8,128)} %copy-done.3) | copy-start | bytes 393220
  526.0 160.2 %all-gather.7.cloned.1.call-start = ((), (), s32[]{:S(2)}) async-start(), calls=%async_computation.4 | async-start | bytes 1949696 | tf_op jit(solution)/shard_map/all_gather | solution.py:65
Sparse Core Ops, SparseCore 0:
  10.1 77.1 all-gather.4
  90.4 72.8 all-reduce.2
  166.7 189.4 all-gather.8
  526.1 76.4 reduce-scatter.1
  618.1 68.0 all-gather.6
